TPU v7x, 32 devices: a whole 2x2x4 slice. The times are simulated.
32 devices in a mesh: group: 2 (over y), batch: 4 (over z), mp: 2 (over x), section: 2 (over core).
Axes of the slice: x: 2, y: 2, z: 4, core: 2. Of those that a mesh axis runs over, the one named last changes fastest.
Arguments:
- queries: bfloat16 [2, 192, 8192], P('section', ('group', 'batch'), 'mp'), parts along dimension 1, may hold values from -6 to 6
- new_keys: bfloat16 [2, 192, 1024], P('section', ('group', 'batch'), 'mp'), parts along dimension 1, may hold values from -6 to 6
- new_values: bfloat16 [2, 192, 1024], P('section', ('group', 'batch'), 'mp'), parts along dimension 1, may hold values from -6 to 6
- key_pages: bfloat16 [2, 768, 16, 1024], P('section', ('group', 'batch'), None, 'mp'), parts along dimension 1, may hold values from -6 to 6
- value_pages: bfloat16 [2, 768, 16, 1024], P('section', ('group', 'batch'), None, 'mp'), parts along dimension 1, may hold values from -6 to 6
- page_table: int32 [192, 4], P(('group', 'batch')), parts along dimension 0, may hold values from 0 to 95, as said below
- ancestry: int32 [192], P('group'), parts along dimension 0, may hold values from 0 to 95, as said below
- lengths: int32 [192], P('group'), parts along dimension 0, may hold values from 1 to 64, as said below
- step_rows: bfloat16 [8192, 4096], P(('group', 'batch', 'section'), 'mp'), parts along dimension 0, may hold values from -6 to 6
- norm_gain: float32 [4096], replicated, may hold values from 0.1 to 1.9
- head_weight: bfloat16 [4096, 4096], P(('batch', 'section'), 'mp'), may hold values from -0.09375 to 0.09375
- head_bias: float32 [4096], P('mp'), may hold values from -5 to 5
- class_weight: bfloat16 [4096, 2], P('mp'), may hold values from -0.125 to 0.125
- class_bias: float32 [2], replicated, may hold values from -4 to 4
Outputs:
- attention: bfloat16 [2, 192, 8192], P('section', ('group', 'batch'), 'mp'), parts along dimension 1
- log_odds: float32 [8192], P(('group', 'batch', 'section')), parts along dimension 0
There are 2 independent parts, one for each index of `group`. A program takes and returns all parts, laid end to end along the dimension named above; an argument that names none is the same for every part. Nothing has to cross between parts.
Inputs may be any that keep to these rules, and one draw needn't show every extreme that they name: The pages of the particles on one index of batch lie on that index; the page_table rows of those 24 particles name each of its 96 pages exactly once. Particle j belongs to problem j % 24, and ancestry[j] % 24 == j % 24. Particles j // 24 == d stand on index d of batch; the 24 slots on one index take at most 12 ancestors from any one index, and in every draw some index gives exactly 12 ancestors to the slots of every index. `lengths`: some particle has all 64 positions live in every draw.
All inputs are finite; a program needn't handle non-finite values.
Results may differ from a plain program's by a relative error of at most 0.0043.
Values may be sent and summed in bfloat16 or wider, within the bound.
A program may use at most 64 MiB of HBM per device.

v0:
```python
import jax
import jax.numpy as jnp
from jax import lax
from jax.sharding import PartitionSpec as P

HD = 128


def cache_score_terms(query_head_count, cached_key_rows, cache_values, live_lengths):
    score_scale = 1.0 / HD**0.5
    attention_scores = (
        jnp.einsum(
            "bkgd,btkd->bkgt", query_head_count, cached_key_rows, preferred_element_type=jnp.float32
        )
        * score_scale
    )
    live_mask = jnp.arange(cached_key_rows.shape[1])[None, :] < live_lengths[:, None]
    attention_scores = jnp.where(live_mask[:, None, None, :], attention_scores, -1e30)
    top_score = jnp.max(attention_scores, axis=-1)
    weights = jnp.exp(attention_scores - top_score[..., None])
    denominator = jnp.sum(weights, axis=-1)
    numerator = jnp.einsum(
        "bkgt,btkd->bkgd",
        weights.astype(jnp.bfloat16),
        cache_values,
        preferred_element_type=jnp.float32,
    )
    return (numerator, top_score, denominator)


def finish(numerator, top_score, denominator, query_head_count, particle_key_rows, own_values):
    score_scale = 1.0 / HD**0.5
    own_score = (
        jnp.einsum(
            "vnrc,vnc->vnr", query_head_count, particle_key_rows, preferred_element_type=jnp.float32
        )
        * score_scale
    )
    own_weight = jnp.exp(own_score - top_score)
    result = (numerator + own_weight[..., None] * own_values.astype(jnp.float32)[:, :, None, :]) / (
        denominator + own_weight
    )[..., None]
    return result.astype(jnp.bfloat16)


def per_device(
    queries,
    new_keys,
    new_values,
    key_pages,
    value_pages,
    page_table,
    ancestry,
    lengths,
    step_rows,
    norm_gain,
    head_weight,
    head_bias,
    class_weight,
    class_bias,
):
    layer_count = queries.shape[0]
    slot_count = page_table.shape[0]
    page_count = page_table.shape[1]
    page_size = key_pages.shape[2]
    kv_width = key_pages.shape[3]
    kv_local = kv_width // HD
    group_size = queries.shape[2] // kv_width
    context = page_count * page_size
    device_count = lax.axis_size("batch")
    my_index = lax.axis_index("batch")
    capacity = max(2, (2 * slot_count + device_count - 1) // device_count)
    source = (ancestry // slot_count).reshape(device_count, slot_count)
    positions = jnp.arange(slot_count)
    earlier = positions[None, :] < positions[:, None]
    same_source = source[:, :, None] == source[:, None, :]
    source_rank = jnp.sum(same_source & earlier[None, :, :], axis=2)
    slot_ids = jnp.arange(capacity)
    served = (source == my_index)[:, None, :] & (source_rank[:, None, :] == slot_ids[None, :, None])
    served_slot = jnp.sum(jnp.where(served, positions[None, None, :], 0), axis=2)
    own_source = lax.dynamic_index_in_dim(source, my_index, 0, keepdims=False)
    own_rank = lax.dynamic_index_in_dim(source_rank, my_index, 0, keepdims=False)
    flat_index = own_source * capacity + own_rank
    local_lengths = lax.dynamic_slice_in_dim(lengths, my_index * slot_count, slot_count)
    query_head_count = queries.reshape(layer_count * slot_count, kv_local, group_size, HD)
    particle_key_rows = new_keys.reshape(layer_count * slot_count, kv_local, HD)
    own_values = new_values.reshape(layer_count * slot_count, kv_local, HD)
    served_pages = page_table[served_slot]
    wanted = (own_source[None, None, :] == jnp.arange(device_count)[:, None, None]) & (
        own_rank[None, None, :] == slot_ids[None, :, None]
    )
    request_slot = jnp.sum(jnp.where(wanted, positions[None, None, :], 0), axis=2)
    outgoing_queries = jnp.take(queries, request_slot, axis=1)
    arrived_queries = lax.all_to_all(
        outgoing_queries, "batch", split_axis=1, concat_axis=1, tiled=True
    )
    batch_rows = layer_count * device_count * capacity
    served_heads = arrived_queries.reshape(batch_rows, kv_local, group_size, HD)
    served_keys = key_pages[:, served_pages].reshape(batch_rows, context, kv_local, HD)
    served_values = value_pages[:, served_pages].reshape(batch_rows, context, kv_local, HD)
    served_lengths = jnp.tile(
        jnp.take(local_lengths, served_slot).reshape(device_count * capacity), layer_count
    )
    numerator, top_score, denominator = cache_score_terms(
        served_heads, served_keys, served_values, served_lengths
    )
    numerator = numerator.reshape(layer_count, device_count, capacity, kv_local * group_size * HD)
    top_score = top_score.reshape(layer_count, device_count, capacity, kv_local * group_size)
    denominator = denominator.reshape(layer_count, device_count, capacity, kv_local * group_size)
    returned = (
        lax.all_to_all(numerator, "batch", split_axis=1, concat_axis=1, tiled=True),
        lax.all_to_all(top_score, "batch", split_axis=1, concat_axis=1, tiled=True),
        lax.all_to_all(denominator, "batch", split_axis=1, concat_axis=1, tiled=True),
    )

    def pick_part(received, trailing):
        received = received.reshape((layer_count, device_count * capacity) + trailing)
        return jnp.take(received, flat_index, axis=1).reshape(
            (layer_count * slot_count,) + trailing
        )

    numerator = pick_part(returned[0], (kv_local, group_size, HD))
    top_score = pick_part(returned[1], (kv_local, group_size))
    denominator = pick_part(returned[2], (kv_local, group_size))
    result = finish(
        numerator, top_score, denominator, query_head_count, particle_key_rows, own_values
    )
    attention = result.reshape(layer_count, slot_count, kv_local * group_size * HD)
    full_rows = lax.all_gather(step_rows, "mp", axis=1, tiled=True)
    row_values = full_rows.astype(jnp.float32)
    power = jnp.mean(row_values * row_values, axis=1, keepdims=True)
    normed = (row_values * lax.rsqrt(power + 1e-06) * norm_gain).astype(jnp.bfloat16)
    projected = jnp.dot(
        normed,
        lax.all_gather(head_weight, ("batch", "section"), axis=0, tiled=True),
        preferred_element_type=jnp.float32,
    )
    hidden = jnp.maximum(projected + head_bias, 0.0).astype(jnp.bfloat16)
    partial_logits = jnp.dot(hidden, class_weight, preferred_element_type=jnp.float32)
    logits = lax.psum(partial_logits, "mp") + class_bias
    log_odds = logits[:, 1] - logits[:, 0]
    return (attention, log_odds)


def solution(mesh):
    placed = (
        P("section", ("group", "batch"), "mp"),
        P("section", ("group", "batch"), "mp"),
        P("section", ("group", "batch"), "mp"),
        P("section", ("group", "batch"), None, "mp"),
        P("section", ("group", "batch"), None, "mp"),
        P(("group", "batch"), None),
        P("group"),
        P("group"),
        P(("group", "batch", "section"), "mp"),
        P(),
        P(("batch", "section"), "mp"),
        P("mp"),
        P("mp", None),
        P(),
    )
    return jax.shard_map(
        per_device,
        mesh=mesh,
        in_specs=placed,
        out_specs=(P("section", ("group", "batch"), "mp"), P(("group", "batch", "section"))),
        check_vma=False,
    )
```

profile of v0, /device:TPU:0, one launch (start us, length us, event | category | flops | bytes accessed | tf_op | source)
XLA Modules:
  0.0 253.1 jit_solution(18221568556298894525)
XLA Ops:
  11.1 0.9 select_bitcast_fusion
  12.0 6.3 %all-to-all-start = ((bf16[1,4,12,4096]{3,2,0,1:T(8,128)(2,1)}), bf16[1,4,12,4096]{3,2,0,1:T(8,128)(2,1)}, u32[]{:S(2)}, u32[]{:S(2)}) async-start(bf16[1,4,12,4096]{3,2,0,1:T(8,128)(2,1)} %select_bitcast_fusion), calls=%async_computation | async-start | bytes 1048576 | tf_op jit(solution)/shard_map/all_to_all | solution.py:94
  20.9 2.7 %gather_fusion.3 = bf16[192,16,512]{2,1,0:T(8,128)(2,1)} fusion(bf16[96,16,512]{2,1,0:T(8,128)(2,1)S(1)} %bitcast.71, s32[1024]{0:T(1024)S(1)} %pad_clamp_fusion.2), kind=kCustom, calls=%fused_computation.5 | custom fusion | bytes 6292224 | tf_op jit(solution)/shard_map/gather | solution.py:99
  23.6 5.6 %reshape.355 = bf16[48,64,4,128]{3,2,1,0:T(4,128)(2,1)} reshape(bf16[192,16,512]{2,1,0:T(8,128)(2,1)} %gather_fusion.3) | data formatting | bytes 6291456 | tf_op jit(solution)/shard_map/reshape | solution.py:99
  29.3 3.6 %all-to-all-done = bf16[1,4,12,4096]{3,2,0,1:T(8,128)(2,1)} async-done(((bf16[1,4,12,4096]{3,2,0,1:T(8,128)(2,1)}), bf16[1,4,12,4096]{3,2,0,1:T(8,128)(2,1)}, u32[]{:S(2)}, u32[]{:S(2)}) %all-to-all-start) | async-done | bytes 393248 | tf_op jit(solution)/shard_map/all_to_all | solution.py:94
  33.0 2.1 reshape.354
  35.0 3.9 %fusion.35 = (f32[48,4,8]{2,1,0:T(4,128)S(1)}, f32[48,4,8,64]{3,2,1,0:T(8,128)S(1)}) fusion(bf16[48,4,8,128]{3,2,1,0:T(8,128)(2,1)} %reshape.354, bf16[48,64,4,128]{3,2,1,0:T(4,128)(2,1)} %reshape.355, pred[48,64]{1,0:T(8,128)(4,1)S(1)} %iota_compare_fusion.1), kind=kOutput, calls=%fused_computation.71 | convolution fusion | flops 25459200 | bytes 3941376 | tf_op jit(solution)/shard_map/bkgd,btkd->bkgt/dot_general | solution.py:12
  41.7 1.5 reduce.4
  43.9 3.2 %all-to-all-start.3 = ((f32[4,1,384]{2,1,0:T(1,128)}), f32[4,1,384]{2,1,0:T(1,128)S(1)}, u32[]{:S(2)}, u32[]{:S(2)}) async-start(f32[4,1,384]{2,1,0:T(1,128)} %reshape.484), calls=%async_computation.3 | async-start | bytes 12288 | tf_op jit(solution)/shard_map/all_to_all | solution.py:113
  47.1 2.7 %gather_fusion.4 = bf16[192,16,512]{2,1,0:T(8,128)(2,1)} fusion(bf16[96,16,512]{2,1,0:T(8,128)(2,1)S(1)} %bitcast.74, s32[1024]{0:T(1024)S(1)} %pad_clamp_fusion.2), kind=kCustom, calls=%fused_computation.6 | custom fusion | bytes 6292224 | tf_op jit(solution)/shard_map/gather | solution.py:100
  49.8 5.6 %reshape.356 = bf16[48,64,4,128]{3,2,1,0:T(4,128)(2,1)} reshape(bf16[192,16,512]{2,1,0:T(8,128)(2,1)} %gather_fusion.4) | data formatting | bytes 6291456 | tf_op jit(solution)/shard_map/reshape | solution.py:100
  57.0 5.0 %all-to-all-start.2 = ((f32[4,1,384]{2,1,0:T(1,128)}), f32[4,1,384]{2,1,0:T(1,128)S(1)}, u32[]{:S(2)}, u32[]{:S(2)}) async-start(f32[4,1,384]{2,1,0:T(1,128)} %reshape.482), calls=%async_computation.2 | async-start | bytes 12288 | tf_op jit(solution)/shard_map/all_to_all | solution.py:112
  62.1 3.8 %fusion.9 = f32[48,4,8,128]{3,2,1,0:T(8,128)} fusion(bf16[48,64,4,128]{3,2,1,0:T(4,128)(2,1)} %reshape.356, f32[48,4,8,64]{3,2,1,0:T(8,128)S(1)} %copy-done.4, f32[48,4,8]{2,1,0:T(4,128)S(1)} %get-tuple-element.9), kind=kOutput, calls=%fused_computation.17 | convolution fusion | flops 25362432 | bytes 4331520 | tf_op jit(solution)/shard_map/bkgt,btkd->bkgd/dot_general | solution.py:22
  65.9 1.8 all-to-all-done.2
  67.6 3.7 %all-to-all-start.1 = ((f32[1,4,12,4096]{3,0,2,1:T(1,128)}), f32[1,4,12,4096]{3,0,2,1:T(1,128)S(1)}, u32[]{:S(2)}, u32[]{:S(2)}) async-start(f32[1,4,12,4096]{3,0,2,1:T(1,128)} %bitcast.8), calls=%async_computation.1 | async-start | bytes 1572864 | tf_op jit(solution)/shard_map/all_to_all | solution.py:111
  75.3 0.9 broadcast_multiply_fusion
  76.2 1.1 mul.82
  77.3 27.7 %all-to-all-done.1 = f32[1,4,12,4096]{3,0,2,1:T(1,128)S(1)} async-done(((f32[1,4,12,4096]{3,0,2,1:T(1,128)}), f32[1,4,12,4096]{3,0,2,1:T(1,128)S(1)}, u32[]{:S(2)}, u32[]{:S(2)}) %all-to-all-start.1) | async-done | bytes 786464 | tf_op jit(solution)/shard_map/all_to_all | solution.py:111
  105.0 1.3 gather_fusion.5
  106.4 1.1 gather.38
  108.3 3.2 %fusion = f32[512]{0:T(512)S(1)} fusion(bf16[512,4096]{1,0:T(8,128)(2,1)} %all-gather.3.cloned.1.call-done), kind=kLoop, calls=%fused_computation.10 | loop fusion | flops 6290944 | bytes 4196352 | tf_op jit(solution)/shard_map/reduce_sum | solution.py:131
  111.5 115.2 %all-gather.5.cloned.1.call-done = bf16[4096,2048]{1,0:T(8,128)(2,1)} async-done(((bf16[512,2048]{1,0:T(8,128)(2,1)}), bf16[4096,2048]{1,0:T(8,128)(2,1)}) %all-gather.5.cloned.1.call-update) | async-done | bytes 16777232 | tf_op jit(solution)/shard_map/all_gather | solution.py:135
  226.6 14.0 %fusion.20 = f32[512,2]{0,1:T(2,128)S(1)} fusion(bf16[2048,2]{0,1:T(2,128)(2,1)S(1)} %copy-done.11, bf16[4096,2048]{1,0:T(8,128)(2,1)} %all-gather.5.cloned.1.call-done, bf16[512,4096]{1,0:T(8,128)(2,1)} %all-gather.3.cloned.1.call-done, f32[4096]{0:T(1024)S(1)} %copy-done.10, f32[512]{0:T(512)S(1)} %add_rsqrt_fusion, f32[2048]{0:T(1024)S(1)} %copy-done.12), kind=kOutput, calls=%fused_computation.23 | convolution fusion | flops 8605663232 | bytes 21010432 | tf_op jit(solution)/shard_map/dot_general | solution.py:139
  240.7 4.9 %psum.7 = f32[512,2]{0,1:T(2,128)S(1)} all-reduce(f32[512,2]{0,1:T(2,128)S(1)} %fusion.20), channel_id=1, replica_groups=mesh['group'=2,'batch'=4,'mp'=2,'section'=2] {'mp'}, use_global_device_ids=true, to_apply=%region_6.8 | all-reduce | flops 1024 | bytes 8192 | tf_op jit(solution)/shard_map/psum | solution.py:140
  (102 shorter events, 16.7 us)
Async XLA Ops:
  7.2 13.7 %copy-start = (bf16[1,96,16,512]{3,2,1,0:T(8,128)(2,1)S(1)}, bf16[1,96,16,512]{3,2,1,0:T(8,128)(2,1)}, u32[]{:S(2)}) copy-start(bf16[1,96,16,512]{3,2,1,0:T(8,128)(2,1)} %param.19) | copy-start | bytes 4718596
  7.2 1.5 copy-start.13
  7.2 3.0 %copy-start.1 = (bf16[1,24,4096]{2,1,0:T(8,128)(2,1)S(1)}, bf16[1,24,4096]{2,1,0:T(8,128)(2,1)}, u32[]{:S(2)}) copy-start(bf16[1,24,4096]{2,1,0:T(8,128)(2,1)} %param.16) | copy-start | bytes 589828
  7.2 101.1 %all-gather.3.cloned.1.call-start = ((), (), s32[]{:S(2)}) async-start(), calls=%async_computation.4 | async-start | bytes 6291456 | tf_op jit(solution)/shard_map/all_gather | solution.py:129
  7.9 218.7 %all-gather.5.cloned.1.call-start = ((), (), s32[]{:S(2)}) async-start(), calls=%async_computation.5 | async-start | bytes 18874368 | tf_op jit(solution)/shard_map/all_gather | solution.py:135
  10.2 8.7 %copy-start.7 = (s32[24,4]{0,1:T(4,128)S(1)}, s32[24,4]{0,1:T(4,128)}, u32[]{:S(2)}) copy-start(s32[24,4]{0,1:T(4,128)} %param.21) | copy-start | bytes 1156
  10.2 9.6 %copy-start.14 = (s32[96]{0:T(128)S(1)}, s32[96]{0:T(128)}, u32[]{:S(2)}) copy-start(s32[96]{0:T(128)} %param.23) | copy-start | bytes 1156
  12.0 20.9 %all-to-all-start = ((bf16[1,4,12,4096]{3,2,0,1:T(8,128)(2,1)}), bf16[1,4,12,4096]{3,2,0,1:T(8,128)(2,1)}, u32[]{:S(2)}, u32[]{:S(2)}) async-start(bf16[1,4,12,4096]{3,2,0,1:T(8,128)(2,1)} %select_bitcast_fusion), calls=%async_computation | async-start | bytes 1048576 | tf_op jit(solution)/shard_map/all_to_all | solution.py:94
  29.3 17.8 %copy-start.2 = (bf16[1,96,16,512]{3,2,1,0:T(8,128)(2,1)S(1)}, bf16[1,96,16,512]{3,2,1,0:T(8,128)(2,1)}, u32[]{:S(2)}) copy-start(bf16[1,96,16,512]{3,2,1,0:T(8,128)(2,1)} %param.20) | copy-start | bytes 4718596
  38.9 0.9 copy-start.3
  43.9 13.1 %all-to-all-start.3 = ((f32[4,1,384]{2,1,0:T(1,128)}), f32[4,1,384]{2,1,0:T(1,128)S(1)}, u32[]{:S(2)}, u32[]{:S(2)}) async-start(f32[4,1,384]{2,1,0:T(1,128)} %reshape.484), calls=%async_computation.3 | async-start | bytes 12288 | tf_op jit(solution)/shard_map/all_to_all | solution.py:113
  49.8 12.2 %copy-start.4 = (f32[48,4,8,64]{3,2,1,0:T(8,128)S(1)}, f32[48,4,8,64]{3,2,1,0:T(8,128)}, u32[]{:S(2)}) copy-start(f32[48,4,8,64]{3,2,1,0:T(8,128)} %copy-done.3) | copy-start | bytes 1179652
  57.0 10.6 %all-to-all-start.2 = ((f32[4,1,384]{2,1,0:T(1,128)}), f32[4,1,384]{2,1,0:T(1,128)S(1)}, u32[]{:S(2)}, u32[]{:S(2)}) async-start(f32[4,1,384]{2,1,0:T(1,128)} %reshape.482), calls=%async_computation.2 | async-start | bytes 12288 | tf_op jit(solution)/shard_map/all_to_all | solution.py:112
  62.1 9.3 %copy-start.5 = (bf16[1,24,512]{2,1,0:T(8,128)(2,1)S(1)}, bf16[1,24,512]{2,1,0:T(8,128)(2,1)}, u32[]{:S(2)}) copy-start(bf16[1,24,512]{2,1,0:T(8,128)(2,1)} %param.17) | copy-start | bytes 73732
  62.1 9.3 %copy-start.6 = (bf16[1,24,512]{2,1,0:T(8,128)(2,1)S(1)}, bf16[1,24,512]{2,1,0:T(8,128)(2,1)}, u32[]{:S(2)}) copy-start(bf16[1,24,512]{2,1,0:T(8,128)(2,1)} %param.18) | copy-start | bytes 73732
  62.1 9.4 %copy-start.8 = (s32[24]{0:T(128)S(1)}, s32[24]{0:T(128)}, u32[]{:S(2)}) copy-start(s32[24]{0:T(128)} %get-tuple-element.6) | copy-start | bytes 292
  67.6 37.4 %all-to-all-start.1 = ((f32[1,4,12,4096]{3,0,2,1:T(1,128)}), f32[1,4,12,4096]{3,0,2,1:T(1,128)S(1)}, u32[]{:S(2)}, u32[]{:S(2)}) async-start(f32[1,4,12,4096]{3,0,2,1:T(1,128)} %bitcast.8), calls=%async_computation.1 | async-start | bytes 1572864 | tf_op jit(solution)/shard_map/all_to_all | solution.py:111
  106.4 120.3 %copy-start.10 = (f32[4096]{0:T(1024)S(1)}, f32[4096]{0:T(1024)}, u32[]{:S(2)}) copy-start(f32[4096]{0:T(1024)} %param.25) | copy-start | bytes 49156
  106.4 120.3 %copy-start.11 = (bf16[2048,2]{0,1:T(2,128)(2,1)S(1)}, bf16[2048,2]{0,1:T(2,128)(2,1)}, u32[]{:S(2)}) copy-start(bf16[2048,2]{0,1:T(2,128)(2,1)} %param.28) | copy-start | bytes 24580
  106.4 120.3 %copy-start.12 = (f32[2048]{0:T(1024)S(1)}, f32[2048]{0:T(1024)}, u32[]{:S(2)}) copy-start(f32[2048]{0:T(1024)} %param.27) | copy-start | bytes 24580
  111.5 134.2 %copy-start.9 = (f32[2]{0:T(128)S(1)}, f32[2]{0:T(128)}, u32[]{:S(2)}) copy-start(f32[2]{0:T(128)} %param.29) | copy-start | bytes 28
Sparse Core Ops, SparseCore 0:
  9.6 59.4 all-gather.2
  70.6 155.9 all-gather.4
where the time goes:
time: 254 us; the launch traced here: 253 us
  waiting for transfers between devices  150 us (59%)
  local copies, waits for them, and re-layouts  31.5 us (12%)
  matrix products  21.9 us (9%)
  starting transfers between devices  18.4 us (7%)
  between operations  14.4 us (6%)
  other arithmetic  12.3 us (5%)
  blocking collectives  4.94 us (2%)
    all_gather x1, waiting for transfers between devices, per_device(): lax.all_gather(head_weight, ('batch', 'section'), axis=0, tiled=True)  115 us
    all_to_all x1, waiting for transfers between devices, per_device(): lax.all_to_all(numerator, 'batch', split_axis=1, concat_axis=1, tiled=True)  27.7 us
    dot_general x1, matrix products, per_device(): jnp.dot(hidden, class_weight, preferred_element_type=jnp.float32)  14 us
    all_to_all x1, starting transfers between devices, per_device(): lax.all_to_all(outgoing_queries, 'batch', split_axis=1, concat_axis=1, ti...  6.35 us
    reshape x1, local copies, waits for them, and re-layouts, per_device(): key_pages[:, served_pages].reshape(batch_rows, context, kv_local, HD)  5.62 us
    reshape x1, local copies, waits for them, and re-layouts, per_device(): value_pages[:, served_pages].reshape(batch_rows, context, kv_local, HD)  5.6 us
  transfers between devices with their start and end apart: 6, of which 4 were waited for; matrix products, arithmetic and copies ran while one was open for 20% of the time, Pallas kernels for 0%

commit v1 on v0

--- a/solution.py
+++ b/solution.py
@@ -4,6 +4,12 @@
 from jax.sharding import PartitionSpec as P
 
 HD = 128
+
+
+def trade_parts(x, mesh_axis, split, join):
+    pieces = jnp.split(x, lax.axis_size(mesh_axis), axis=split)
+    received = lax.all_to_all(jnp.stack(pieces), mesh_axis, 0, 0)
+    return jnp.concatenate(received, axis=join)
 
 
 def cache_score_terms(query_head_count, cached_key_rows, cache_values, live_lengths):
@@ -108,7 +114,7 @@
     top_score = top_score.reshape(layer_count, device_count, capacity, kv_local * group_size)
     denominator = denominator.reshape(layer_count, device_count, capacity, kv_local * group_size)
     returned = (
-        lax.all_to_all(numerator, "batch", split_axis=1, concat_axis=1, tiled=True),
+        trade_parts(numerator, "batch", 1, 1),
         lax.all_to_all(top_score, "batch", split_axis=1, concat_axis=1, tiled=True),
         lax.all_to_all(denominator, "batch", split_axis=1, concat_axis=1, tiled=True),
     )

time: 254 us -> 254 us (level)
  waiting for transfers between devices: 150 us -> 146 us
    all_to_all x1, waiting for transfers between devices: 3.65 us -> 0.01 us  [per_device(): lax.all_to_all(outgoing_queries, 'batch', split_axis=1, concat_axis=1, ti...]
    another operation x0 -> x2, local copies, waits for them, and re-layouts: none -> 2.65 us  [trade_parts(): received = lax.all_to_all(jnp.stack(pieces), mesh_axis, 0, 0)]
  transfers between devices with their start and end apart: 6 -> 6, of which waited for: 4 -> 3; matrix products, arithmetic and copies ran while one was open for 20% -> 21% of each run, Pallas kernels for 0% -> 0%
where the time goes in v1:
time: 254 us; the launch traced here: 253 us
  waiting for transfers between devices  146 us (57%)
  local copies, waits for them, and re-layouts  33.3 us (13%)
  matrix products  21.8 us (9%)
  starting transfers between devices  20.3 us (8%)
  between operations  14.4 us (6%)
  other arithmetic  12 us (5%)
  blocking collectives  4.94 us (2%)
    all_gather x1, waiting for transfers between devices, per_device(): lax.all_gather(head_weight, ('batch', 'section'), axis=0, tiled=True)  114 us
    all_to_all x1, waiting for transfers between devices, trade_parts(): received = lax.all_to_all(jnp.stack(pieces), mesh_axis, 0, 0)  27.7 us
    dot_general x1, matrix products, per_device(): jnp.dot(hidden, class_weight, preferred_element_type=jnp.float32)  14 us
    all_to_all x1, starting transfers between devices, per_device(): lax.all_to_all(outgoing_queries, 'batch', split_axis=1, concat_axis=1, ti...  6.35 us
    reshape x1, local copies, waits for them, and re-layouts, per_device(): value_pages[:, served_pages].reshape(batch_rows, context, kv_local, HD)  5.75 us
    reshape x1, local copies, waits for them, and re-layouts, per_device(): key_pages[:, served_pages].reshape(batch_rows, context, kv_local, HD)  5.53 us
    all_to_all x1, starting transfers between devices, per_device(): lax.all_to_all(top_score, 'batch', split_axis=1, concat_axis=1, tiled=True)  5.09 us
    all_to_all x1, starting transfers between devices, per_device(): lax.all_to_all(denominator, 'batch', split_axis=1, concat_axis=1, tiled=T...  5.09 us
  transfers between devices with their start and end apart: 6, of which 3 were waited for; matrix products, arithmetic and copies ran while one was open for 21% of the time, Pallas kernels for 0%

profile of v1, /device:TPU:0, one launch (start us, length us, event | category | flops | bytes accessed | tf_op | source)
XLA Modules:
  0.0 253.0 jit_solution(4023877899823016515)
XLA Ops:
  10.6 0.9 select_bitcast_fusion
  11.5 6.3 %all-to-all-start = ((bf16[1,4,12,4096]{3,2,0,1:T(8,128)(2,1)}), bf16[1,4,12,4096]{3,2,0,1:T(8,128)(2,1)}, u32[]{:S(2)}, u32[]{:S(2)}) async-start(bf16[1,4,12,4096]{3,2,0,1:T(8,128)(2,1)} %select_bitcast_fusion), calls=%async_computation | async-start | bytes 1048576 | tf_op jit(solution)/shard_map/all_to_all | solution.py:100
  20.4 2.7 %gather_fusion.4 = bf16[192,16,512]{2,1,0:T(8,128)(2,1)} fusion(bf16[96,16,512]{2,1,0:T(8,128)(2,1)S(1)} %bitcast.80, s32[1024]{0:T(1024)S(1)} %pad_clamp_fusion.2), kind=kCustom, calls=%fused_computation.6 | custom fusion | bytes 6292224 | tf_op jit(solution)/shard_map/gather | solution.py:106
  23.1 5.8 %reshape.353 = bf16[48,64,4,128]{3,2,1,0:T(4,128)(2,1)} reshape(bf16[192,16,512]{2,1,0:T(8,128)(2,1)} %gather_fusion.4) | data formatting | bytes 6291456 | tf_op jit(solution)/shard_map/reshape | solution.py:106
  28.9 2.7 %gather_fusion.3 = bf16[192,16,512]{2,1,0:T(8,128)(2,1)} fusion(bf16[96,16,512]{2,1,0:T(8,128)(2,1)S(1)} %bitcast.83, s32[1024]{0:T(1024)S(1)} %pad_clamp_fusion.2), kind=kCustom, calls=%fused_computation.5 | custom fusion | bytes 6292224 | tf_op jit(solution)/shard_map/gather | solution.py:105
  31.6 5.5 %reshape.352 = bf16[48,64,4,128]{3,2,1,0:T(4,128)(2,1)} reshape(bf16[192,16,512]{2,1,0:T(8,128)(2,1)} %gather_fusion.3) | data formatting | bytes 6291456 | tf_op jit(solution)/shard_map/reshape | solution.py:105
  37.2 1.3 reshape.351
  38.6 3.7 %fusion.35 = (f32[48,4,8]{2,1,0:T(4,128)S(1)}, f32[48,4,8,64]{3,2,1,0:T(8,128)S(1)}) fusion(bf16[48,4,8,128]{3,2,1,0:T(8,128)(2,1)S(1)} %reshape.351, bf16[48,64,4,128]{3,2,1,0:T(4,128)(2,1)} %reshape.352, pred[48,64]{1,0:T(8,128)(4,1)S(1)} %iota_compare_fusion.1), kind=kOutput, calls=%fused_computation.76 | convolution fusion | flops 25459200 | bytes 3941376 | tf_op jit(solution)/shard_map/bkgd,btkd->bkgt/dot_general | solution.py:18
  44.9 5.1 %all-to-all-start.3 = ((f32[4,1,384]{2,1,0:T(1,128)}), f32[4,1,384]{2,1,0:T(1,128)S(1)}, u32[]{:S(2)}, u32[]{:S(2)}) async-start(f32[4,1,384]{2,1,0:T(1,128)} %reshape.480), calls=%async_computation.3 | async-start | bytes 12288 | tf_op jit(solution)/shard_map/all_to_all | solution.py:119
  50.0 3.8 %fusion.9 = f32[48,4,8,128]{3,2,1,0:T(8,128)} fusion(bf16[48,64,4,128]{3,2,1,0:T(4,128)(2,1)} %reshape.353, f32[48,4,8,64]{3,2,1,0:T(8,128)S(1)} %get-tuple-element.14, f32[48,4,8]{2,1,0:T(4,128)S(1)} %get-tuple-element.13), kind=kOutput, calls=%fused_computation.17 | convolution fusion | flops 25362432 | bytes 4331520 | tf_op jit(solution)/shard_map/bkgt,btkd->bkgd/dot_general | solution.py:28
  53.8 1.3 reshape.354
  57.5 5.1 %all-to-all-start.2 = ((f32[4,1,384]{2,1,0:T(1,128)}), f32[4,1,384]{2,1,0:T(1,128)S(1)}, u32[]{:S(2)}, u32[]{:S(2)}) async-start(f32[4,1,384]{2,1,0:T(1,128)} %reshape.478), calls=%async_computation.2 | async-start | bytes 12288 | tf_op jit(solution)/shard_map/all_to_all | solution.py:118
  62.5 1.1 pad_maximum_fusion
  63.6 1.8 copy.60
  65.4 2.7 %all-to-all-done.2 = f32[4,1,384]{2,1,0:T(1,128)S(1)} async-done(((f32[4,1,384]{2,1,0:T(1,128)}), f32[4,1,384]{2,1,0:T(1,128)S(1)}, u32[]{:S(2)}, u32[]{:S(2)}) %all-to-all-start.2) | async-done | bytes 6176 | tf_op jit(solution)/shard_map/all_to_all | solution.py:118
  68.1 3.7 %all-to-all-start.1 = ((f32[4,1,1,12,4096]{4,2,3,1,0:T(1,128)}), f32[4,1,1,12,4096]{4,2,3,1,0:T(1,128)S(1)}, u32[]{:S(2)}, u32[]{:S(2)}) async-start(f32[4,1,1,12,4096]{4,2,3,1,0:T(1,128)} %copy.60), calls=%async_computation.1 | async-start | bytes 1572864 | tf_op jit(solution)/shard_map/all_to_all | solution.py:11
  76.6 1.1 mul.82
  77.7 27.7 %all-to-all-done.1 = f32[4,1,1,12,4096]{4,2,3,1,0:T(1,128)S(1)} async-done(((f32[4,1,1,12,4096]{4,2,3,1,0:T(1,128)}), f32[4,1,1,12,4096]{4,2,3,1,0:T(1,128)S(1)}, u32[]{:S(2)}, u32[]{:S(2)}) %all-to-all-start.1) | async-done | bytes 786464 | tf_op jit(solution)/shard_map/all_to_all | solution.py:11
  105.5 1.3 gather_fusion.5
  106.8 1.3 gather.38
  108.9 3.1 %fusion = f32[512]{0:T(512)S(1)} fusion(bf16[512,4096]{1,0:T(8,128)(2,1)} %all-gather.3.cloned.1.call-done), kind=kLoop, calls=%fused_computation.10 | loop fusion | flops 6290944 | bytes 4196352 | tf_op jit(solution)/shard_map/reduce_sum | solution.py:137
  112.0 114.5 %all-gather.5.cloned.1.call-done = bf16[4096,2048]{1,0:T(8,128)(2,1)} async-done(((bf16[512,2048]{1,0:T(8,128)(2,1)}), bf16[4096,2048]{1,0:T(8,128)(2,1)}) %all-gather.5.cloned.1.call-update) | async-done | bytes 16777232 | tf_op jit(solution)/shard_map/all_gather | solution.py:141
  226.5 14.0 %fusion.20 = f32[512,2]{0,1:T(2,128)S(1)} fusion(bf16[2048,2]{0,1:T(2,128)(2,1)S(1)} %copy-done.8, bf16[4096,2048]{1,0:T(8,128)(2,1)} %all-gather.5.cloned.1.call-done, bf16[512,4096]{1,0:T(8,128)(2,1)} %all-gather.3.cloned.1.call-done, f32[4096]{0:T(1024)S(1)} %copy-done.7, f32[512]{0:T(512)S(1)} %add_rsqrt_fusion, f32[2048]{0:T(1024)S(1)} %copy-done.9), kind=kOutput, calls=%fused_computation.23 | convolution fusion | flops 8605663232 | bytes 21010432 | tf_op jit(solution)/shard_map/dot_general | solution.py:145
  240.6 4.9 %psum.7 = f32[512,2]{0,1:T(2,128)S(1)} all-reduce(f32[512,2]{0,1:T(2,128)S(1)} %fusion.20), channel_id=1, replica_groups=mesh['group'=2,'batch'=4,'mp'=2,'section'=2] {'mp'}, use_global_device_ids=true, to_apply=%region_6.8 | all-reduce | flops 1024 | bytes 8192 | tf_op jit(solution)/shard_map/psum | solution.py:146
  (100 shorter events, 17.0 us)
Async XLA Ops:
  7.2 13.2 %copy-start = (bf16[1,96,16,512]{3,2,1,0:T(8,128)(2,1)S(1)}, bf16[1,96,16,512]{3,2,1,0:T(8,128)(2,1)}, u32[]{:S(2)}) copy-start(bf16[1,96,16,512]{3,2,1,0:T(8,128)(2,1)} %param.20) | copy-start | bytes 4718596
  7.2 1.5 copy-start.10
  7.2 2.5 copy-start.1
  7.2 101.7 %all-gather.3.cloned.1.call-start = ((), (), s32[]{:S(2)}) async-start(), calls=%async_computation.4 | async-start | bytes 6291456 | tf_op jit(solution)/shard_map/all_gather | solution.py:135
  7.9 218.6 %all-gather.5.cloned.1.call-start = ((), (), s32[]{:S(2)}) async-start(), calls=%async_computation.5 | async-start | bytes 18874368 | tf_op jit(solution)/shard_map/all_gather | solution.py:141
  9.7 8.7 %copy-start.5 = (s32[24,4]{0,1:T(4,128)S(1)}, s32[24,4]{0,1:T(4,128)}, u32[]{:S(2)}) copy-start(s32[24,4]{0,1:T(4,128)} %param.21) | copy-start | bytes 1156
  9.7 9.6 %copy-start.11 = (s32[96]{0:T(128)S(1)}, s32[96]{0:T(128)}, u32[]{:S(2)}) copy-start(s32[96]{0:T(128)} %param.23) | copy-start | bytes 1156
  11.5 25.7 %all-to-all-start = ((bf16[1,4,12,4096]{3,2,0,1:T(8,128)(2,1)}), bf16[1,4,12,4096]{3,2,0,1:T(8,128)(2,1)}, u32[]{:S(2)}, u32[]{:S(2)}) async-start(bf16[1,4,12,4096]{3,2,0,1:T(8,128)(2,1)} %select_bitcast_fusion), calls=%async_computation | async-start | bytes 1048576 | tf_op jit(solution)/shard_map/all_to_all | solution.py:100
  23.1 5.8 %copy-start.2 = (bf16[1,96,16,512]{3,2,1,0:T(8,128)(2,1)S(1)}, bf16[1,96,16,512]{3,2,1,0:T(8,128)(2,1)}, u32[]{:S(2)}) copy-start(bf16[1,96,16,512]{3,2,1,0:T(8,128)(2,1)} %param.19) | copy-start | bytes 4718596
  44.9 12.5 %all-to-all-start.3 = ((f32[4,1,384]{2,1,0:T(1,128)}), f32[4,1,384]{2,1,0:T(1,128)S(1)}, u32[]{:S(2)}, u32[]{:S(2)}) async-start(f32[4,1,384]{2,1,0:T(1,128)} %reshape.480), calls=%async_computation.3 | async-start | bytes 12288 | tf_op jit(solution)/shard_map/all_to_all | solution.py:119
  55.9 15.9 %copy-start.3 = (bf16[1,24,512]{2,1,0:T(8,128)(2,1)S(1)}, bf16[1,24,512]{2,1,0:T(8,128)(2,1)}, u32[]{:S(2)}) copy-start(bf16[1,24,512]{2,1,0:T(8,128)(2,1)} %param.17) | copy-start | bytes 73732
  55.9 15.9 %copy-start.4 = (bf16[1,24,512]{2,1,0:T(8,128)(2,1)S(1)}, bf16[1,24,512]{2,1,0:T(8,128)(2,1)}, u32[]{:S(2)}) copy-start(bf16[1,24,512]{2,1,0:T(8,128)(2,1)} %param.18) | copy-start | bytes 73732
  57.5 10.7 %all-to-all-start.2 = ((f32[4,1,384]{2,1,0:T(1,128)}), f32[4,1,384]{2,1,0:T(1,128)S(1)}, u32[]{:S(2)}, u32[]{:S(2)}) async-start(f32[4,1,384]{2,1,0:T(1,128)} %reshape.478), calls=%async_computation.2 | async-start | bytes 12288 | tf_op jit(solution)/shard_map/all_to_all | solution.py:118
  68.1 37.3 %all-to-all-start.1 = ((f32[4,1,1,12,4096]{4,2,3,1,0:T(1,128)}), f32[4,1,1,12,4096]{4,2,3,1,0:T(1,128)S(1)}, u32[]{:S(2)}, u32[]{:S(2)}) async-start(f32[4,1,1,12,4096]{4,2,3,1,0:T(1,128)} %copy.60), calls=%async_computation.1 | async-start | bytes 1572864 | tf_op jit(solution)/shard_map/all_to_all | solution.py:11
  106.8 119.7 %copy-start.7 = (f32[4096]{0:T(1024)S(1)}, f32[4096]{0:T(1024)}, u32[]{:S(2)}) copy-start(f32[4096]{0:T(1024)} %param.25) | copy-start | bytes 49156
  106.8 119.7 %copy-start.8 = (bf16[2048,2]{0,1:T(2,128)(2,1)S(1)}, bf16[2048,2]{0,1:T(2,128)(2,1)}, u32[]{:S(2)}) copy-start(bf16[2048,2]{0,1:T(2,128)(2,1)} %param.28) | copy-start | bytes 24580
  106.8 119.7 %copy-start.9 = (f32[2048]{0:T(1024)S(1)}, f32[2048]{0:T(1024)}, u32[]{:S(2)}) copy-start(f32[2048]{0:T(1024)} %param.27) | copy-start | bytes 24580
  112.0 133.5 %copy-start.6 = (f32[2]{0:T(128)S(1)}, f32[2]{0:T(128)}, u32[]{:S(2)}) copy-start(f32[2]{0:T(128)} %param.29) | copy-start | bytes 28
Sparse Core Ops, SparseCore 0:
  9.6 59.4 all-gather.2
  70.6 155.8 all-gather.4
